TPU v7x, 32 devices: a whole 2x2x4 slice. The times are simulated.
32 devices in a mesh: space: 16 (over z, y, core), chan: 2 (over x).
Axes of the slice: x: 2, y: 2, z: 4, core: 2. Of those that a mesh axis runs over, the one named last changes fastest.
Arguments:
- volume: float32 [32, 32, 128, 128], P('chan', 'space'), may hold values from -6 to 6
- filters: float32 [64, 32, 3, 3, 3], P(None, 'chan'), may hold values from -0.21875 to 0.21875
- cotangent: float32 [64, 16, 64, 64], P('chan', 'space'), may hold values from -6 to 6
Outputs:
- activated: float32 [64, 16, 64, 64], P('chan', 'space')
- volume_grad: float32 [32, 32, 128, 128], P('chan', 'space')
- filter_grad: float32 [64, 32, 3, 3, 3], P(None, 'chan')
All inputs are finite; a program needn't handle non-finite values.
Results may differ from a plain program's by a relative error of at most 0.00014.
Values sent between devices are 32-bit elements; how exact they have to be, the bound alone decides.
No kernel may reach another device: no remote copies, remote signals or barrier semaphores. Data moves between devices by JAX's collectives and lax.ppermute only.
A program may use at most 192 MiB of HBM per device.

v0:
```python
import jax
import jax.numpy as jnp
from jax import lax
from jax.sharding import PartitionSpec as P


def from_behind(value, axis, steps):
    count = lax.axis_size(axis)
    initial, last = (max(0, -steps), min(count, count - steps))
    return lax.ppermute(value, axis, [(source, source + steps) for source in range(initial, last)])


def conv_local(extended, filters):
    result = lax.conv_general_dilated(
        extended[None],
        filters,
        (2, 2, 2),
        ((0, 0), (1, 1), (1, 1)),
        dimension_numbers=("NCDHW", "OIDHW", "NCDHW"),
        precision=lax.Precision.HIGHEST,
    )
    return result[0]


def on_device(volume, filters, cotangent):
    out_rows = cotangent.shape[0]
    top_plane = volume[:, -1]
    below = from_behind(top_plane, "space", 1)
    extended = jnp.concatenate([below[:, None], volume], axis=1)
    every_filter = lax.all_gather(filters, "chan", axis=1, tiled=True)
    own_filters = lax.dynamic_slice_in_dim(
        every_filter, lax.axis_index("chan") * out_rows, out_rows, 0
    )
    initial = jnp.zeros(cotangent.shape, jnp.float32)
    chosen = own_filters
    preact = initial + conv_local(lax.all_gather(extended, "chan", axis=0, tiled=True), chosen)
    activated = jax.nn.softplus(preact)
    preact_grad = cotangent * jax.nn.sigmoid(preact)
    piece = lax.all_gather(preact_grad, "chan", axis=0, tiled=True)
    start = jnp.int32(0)
    grad_filters = jnp.zeros(filters.shape, jnp.float32)
    chosen = lax.dynamic_slice_in_dim(filters, start, piece.shape[0], 0)
    unused, pullback = jax.vjp(conv_local, extended, chosen)
    grad_piece, grad_rows = pullback(piece)
    grad_extended, grad_filters = (
        grad_piece,
        lax.dynamic_update_slice_in_dim(grad_filters, grad_rows, start, 0),
    )
    spilled = from_behind(grad_extended[:, 0], "space", -1)
    volume_grad = grad_extended[:, 1:]
    volume_grad = volume_grad.at[:, -1].add(spilled)
    summed = lax.psum(grad_filters, "space")
    depth_all = volume.shape[1] * lax.axis_size("space")
    factor = float(depth_all // 2 * (volume.shape[2] // 2) * (volume.shape[3] // 2)) ** (-0.5)
    return (activated, volume_grad, summed * factor)


def solution(mesh):
    in_specs = (
        P("chan", "space", None, None),
        P(None, "chan", None, None, None),
        P("chan", "space", None, None),
    )
    out_specs = (
        P("chan", "space", None, None),
        P("chan", "space", None, None),
        P(None, "chan", None, None, None),
    )
    return jax.shard_map(
        on_device, mesh=mesh, in_specs=in_specs, out_specs=out_specs, check_vma=False
    )
```

profile of v0, /device:TPU:8, one launch (start us, length us, event | category | flops | bytes accessed | tf_op | source)
XLA Modules:
  0.0 647.2 jit_solution(8381787127257969497)
XLA Ops:
  7.2 2.4 slice_bitcast_fusion.3
  11.6 8.6 %copy.48 = f32[16,2,128,128]{0,3,2,1:T(8,128)} copy(f32[16,2,128,128]{3,2,1,0:T(8,128)S(1)} %copy-done) | data formatting | bytes 4194304 | tf_op args[0]
  20.1 6.7 %collective-permute-done = f32[16,128,128]{2,1,0:T(8,128)S(1)} collective-permute-done((f32[16,128,128]{2,1,0:T(8,128)}, f32[16,128,128]{2,1,0:T(8,128)S(1)}, u32[]{:S(2)}, u32[]{:S(2)}) %collective-permute-start) | collective-permute-done | bytes 1048608 | tf_op jit(solution)/shard_map/ppermute | solution.py:10
  26.9 4.6 copy.47
  31.5 18.6 %pad_maximum_fusion = f32[16,3,128,128]{0,3,2,1:T(8,128)} fusion(f32[16,2,128,128]{0,3,2,1:T(8,128)} %copy.48, f32[16,1,128,128]{0,3,2,1:T(8,128)} %bitcast.46), kind=kLoop, calls=%fused_computation.6 | loop fusion | flops 786432 | bytes 6291456 | tf_op jit(solution)/shard_map/concatenate | solution.py:29
  50.1 16.0 %copy.49 = f32[16,3,128,128]{3,2,1,0:T(8,128)} copy(f32[16,3,128,128]{0,3,2,1:T(8,128)} %pad_maximum_fusion) | data formatting | bytes 6291456 | tf_op jit(solution)/shard_map/concatenate | solution.py:29
  68.2 7.1 %all_gather.10 = f32[64,32,3,3,3]{0,1,4,3,2:T(8,128)S(1)} all-gather(f32[64,16,3,3,3]{0,1,4,3,2:T(8,128)S(1)} %copy-done.2), channel_id=1, replica_groups=mesh['space'=16,'chan'=2] {'chan'}, dimensions={1}, use_global_device_ids=true | all-gather | bytes 331776 | tf_op jit(solution)/shard_map/all_gather | solution.py:30
  75.3 71.6 %all-gather.3.cloned.1.call-done = f32[32,3,128,128]{3,2,1,0:T(8,128)} async-done(((f32[16,3,128,128]{3,2,1,0:T(8,128)}), f32[32,3,128,128]{3,2,1,0:T(8,128)}) %all-gather.3.cloned.1.call-update) | async-done | bytes 6291472 | tf_op jit(solution)/shard_map/all_gather | solution.py:36
  146.9 6.7 %copy.50 = f32[32,3,128,128]{2,0,3,1:T(8,128)} copy(f32[32,3,128,128]{3,2,1,0:T(8,128)} %all-gather.3.cloned.1.call-done) | data formatting | bytes 12582912 | tf_op jit(solution)/shard_map/all_gather | solution.py:36
  153.6 6.7 %pad.2 = f32[32,3,128,1,144]{2,0,4,1,3:T(8,128)} pad(f32[32,3,128,1,128]{2,0,4,1,3:T(8,128)} %bitcast.48, f32[]{:T(128)} %constant.42.clone.1), padding=0_0x0_0x0_0x0_0x1_15 | pad | bytes 13369348 | tf_op jit(solution)/shard_map/broadcast_in_dim | solution.py:15
  160.3 24.8 %copy.52 = f32[32,3,128,1,8,18]{0,4,5,2,1,3:T(8,128)} copy(f32[32,3,128,1,8,18]{2,0,5,4,1,3:T(8,128)} %bitcast.47) | data formatting | bytes 14155776 | tf_op jit(solution)/shard_map/conv_general_dilated | solution.py:14
  187.3 37.1 %fusion.11 = f32[1,64,8,9,32]{4,2,3,1,0:T(8,128)} fusion(f32[32,3,128,1,7,2]{0,4,5,2,1,3:T(8,128)S(1)} %slice.45, f32[32,3,128,1,8,18]{0,4,5,2,1,3:T(8,128)} %copy.52, pred[8,9]{0,1:T(8,128)(4,1)S(1)} %copy-done.4, f32[64,32,3,3,3]{0,1,4,3,2:T(8,128)S(1)} %all_gather.10, s32[]{:T(128)S(6)} %select_n.15), kind=kOutput, calls=%fused_computation.17 | convolution fusion | flops 1526906880 | bytes 8577100 | tf_op jit(solution)/shard_map/conv_general_dilated | solution.py:14
  230.0 33.2 %all-gather.5.cloned.1.call-done = f32[64,1,64,64]{3,2,1,0:T(8,128)} async-done(((f32[32,1,64,64]{3,2,1,0:T(8,128)}), f32[64,1,64,64]{3,2,1,0:T(8,128)}) %all-gather.5.cloned.1.call-update) | async-done | bytes 1048592 | tf_op jit(solution)/shard_map/all_gather | solution.py:39
  263.3 3.1 copy.57
  268.0 2.3 copy.59
  271.0 86.4 %broadcast_select_fusion = f32[3,128,8,18,16]{4,2,3,1,0:T(8,128)} fusion(pred[8,18]{0,1:T(8,128)(4,1)S(1)} %copy-done.3, f32[64,16,3,3,3]{0,1,4,3,2:T(8,128)S(1)} %copy-done.2, f32[64,1,64,8,10]{0,3,4,2,1:T(8,128)S(1)} %fusion.32), kind=kOutput, calls=%fused_computation.9 | convolution fusion | flops 1521745920 | bytes 4960400 | tf_op jit(solution)/shard_map/transpose(jvp())/conv_general_dilated | solution.py:14
  357.4 17.2 %copy.60 = f32[3,128,8,18,16]{1,4,3,2,0:T(8,128)} copy(f32[3,128,8,18,16]{4,2,3,1,0:T(8,128)} %broadcast_select_fusion) | data formatting | bytes 7077888 | tf_op jit(solution)/shard_map/transpose(jvp())/conv_general_dilated | solution.py:14
  377.8 2.8 collective-permute-start.1
  380.6 3.3 copy.61
  383.9 159.1 %fusion.25 = f32[64,16,3,3,3]{0,1,4,3,2:T(8,128)} fusion(f32[1,16,3,128,128]{1,0,4,3,2:T(1,128)} %bitcast.45, f32[1,64,1,64,64]{1,0,4,3,2:T(1,128)} %bitcast.53), kind=kOutput, calls=%fused_computation.35 | convolution fusion | flops 1344835584 | bytes 4304896 | tf_op jit(solution)/shard_map/transpose(jvp())/conv_general_dilated | solution.py:14
  543.1 2.7 copy.62
  547.3 86.3 %all-reduce.2.cloned.1.call-done = f32[64,16,3,3,3]{0,1,4,3,2:T(8,128)} async-done(((f32[64,16,3,3,3]{0,1,4,3,2:T(8,128)}), f32[64,16,3,3,3]{0,1,4,3,2:T(8,128)}) %all-reduce.2.cloned.1.call-update) | async-done | bytes 110608 | tf_op jit(solution)/shard_map/psum | solution.py:52
  635.2 2.4 fusion.16
  637.6 2.9 copy.63
  (30 shorter events, 20.5 us)
Async XLA Ops:
  7.2 4.4 copy-start
  7.2 139.7 %all-gather.3.cloned.1.call-start = ((), (), s32[]{:S(2)}) async-start(), calls=%async_computation | async-start | bytes 9437184 | tf_op jit(solution)/shard_map/all_gather | solution.py:36
  9.7 17.2 %collective-permute-start = (f32[16,128,128]{2,1,0:T(8,128)}, f32[16,128,128]{2,1,0:T(8,128)S(1)}, u32[]{:S(2)}, u32[]{:S(2)}) collective-permute-start(f32[16,128,128]{2,1,0:T(8,128)} %slice_bitcast_fusion.3), channel_id=1, source_target_pairs={{0,2},{2,4},{4,6},{6,8},{8,10},{10,12},{12,14},{14,16},{16,18},{18... | collective-permute-start | bytes 3145736 | tf_op jit(solution)/shard_map/ppermute | solution.py:10
  66.1 1.2 copy-start.1
  66.1 2.2 copy-start.2
  66.1 197.2 %all-gather.5.cloned.1.call-start = ((), (), s32[]{:S(2)}) async-start(), calls=%async_computation.1 | async-start | bytes 3145728 | tf_op jit(solution)/shard_map/all_gather | solution.py:39
  185.1 2.2 copy-start.4
  230.0 403.6 %all-reduce.2.cloned.1.call-start = ((), (), s32[]{:S(2)}) async-start(), calls=%async_computation.2 | async-start | bytes 442368 | tf_op jit(solution)/shard_map/psum | solution.py:52
  270.3 0.7 copy-start.3
  377.8 257.4 %collective-permute-start.1 = (f32[16,128,128]{1,0,2:T(8,128)}, f32[16,128,128]{1,0,2:T(8,128)}, u32[]{:S(2)}, u32[]{:S(2)}) collective-permute-start(f32[16,128,128]{1,0,2:T(8,128)} %slice_bitcast_fusion.1), channel_id=1, source_target_pairs={{2,0},{4,2},{6,4},{8,6},{10,8},{12,10},{14,12},{16,14},{18,16},{20... | collective-permute-start | bytes 3145736 | tf_op jit(solution)/shard_map/ppermute | solution.py:10
Sparse Core Ops, SparseCore 0:
  66.2 80.6 all-gather.2
  230.1 33.1 all-gather.4
  543.2 90.3 all-reduce.1
where the time goes:
time: 651 us; the launch traced here: 647 us
  matrix products  283 us (43%)
  waiting for transfers between devices  198 us (30%)
  local copies, waits for them, and re-layouts  116 us (18%)
  other arithmetic  24.5 us (4%)
  between operations  14.1 us (2%)
  blocking collectives  7.07 us (1%)
    conv_general_dilated x3, matrix products, conv_local(): lax.conv_general_dilated(extended[None], filters, (2, 2, 2), ((0, 0), (1,...  283 us
    psum x1, waiting for transfers between devices, on_device(): summed = lax.psum(grad_filters, 'space')  86.3 us
    all_gather x1, waiting for transfers between devices, on_device(): lax.all_gather(extended, 'chan', axis=0, tiled=True)  71.6 us
    conv_general_dilated x6, local copies, waits for them, and re-layouts, conv_local(): lax.conv_general_dilated(extended[None], filters, (2, 2, 2), ((0, 0), (1,...  48.8 us
    all_gather x1, waiting for transfers between devices, on_device(): piece = lax.all_gather(preact_grad, 'chan', axis=0, tiled=True)  33.2 us
    concatenate x1, other arithmetic, on_device(): extended = jnp.concatenate([below[:, None], volume], axis=1)  18.6 us
    unnamed x14, local copies, waits for them, and re-layouts  16.7 us
    concatenate x1, local copies, waits for them, and re-layouts, on_device(): extended = jnp.concatenate([below[:, None], volume], axis=1)  16 us
  transfers between devices with their start and end apart: 5, of which 4 were waited for; matrix products, arithmetic and copies ran while one was open for 27% of the time, Pallas kernels for 0%

commit v1 on v0

--- a/solution.py
+++ b/solution.py
@@ -1,7 +1,29 @@
+import functools
 import jax
 import jax.numpy as jnp
 from jax import lax
 from jax.sharding import PartitionSpec as P
+from jax.lax import axis_index, axis_size, ppermute
+
+
+def apply_the_slots(frame_in, dim_i):
+    state_next = axis_index("chan")
+    response = axis_size("chan")
+    arr_out, z2 = (response, state_next)
+    after, r_now = (frame_in, 1)
+    while r_now < arr_out:
+        u_next = range(arr_out)
+        earlier = map(lambda j0: (j0, j0 ^ r_now), u_next)
+        z = list(earlier)
+        a_now = ppermute(after, "chan", z)
+        state_now = jnp.concatenate([after, a_now], axis=dim_i)
+        new = jnp.concatenate([a_now, after], axis=dim_i)
+        after = jnp.where(z2 & r_now == 0, state_now, new)
+        r_now = 2 * r_now
+    return after
+
+
+_answer_shards = functools.partial(apply_the_slots, dim_i=0)
 
 
 def from_behind(value, axis, steps):
@@ -33,7 +55,7 @@
     )
     initial = jnp.zeros(cotangent.shape, jnp.float32)
     chosen = own_filters
-    preact = initial + conv_local(lax.all_gather(extended, "chan", axis=0, tiled=True), chosen)
+    preact = initial + conv_local(_answer_shards(extended), chosen)
     activated = jax.nn.softplus(preact)
     preact_grad = cotangent * jax.nn.sigmoid(preact)
     piece = lax.all_gather(preact_grad, "chan", axis=0, tiled=True)

time: 651 us -> 788 us (1.21)
  other arithmetic: 24.5 us -> 136 us
  waiting for transfers between devices: 198 us -> 126 us
  blocking collectives: 7.07 us -> 70.9 us
  local copies, waits for them, and re-layouts: 116 us -> 143 us
    select_n x0 -> x1, other arithmetic: none -> 112 us  [apply_the_slots(): after = jnp.where(z2 & r_now == 0, state_now, new)]
    all_gather x1 -> x0, waiting for transfers between devices: 71.6 us -> none  [on_device(): lax.all_gather(extended, 'chan', axis=0, tiled=True)]
    all_gather x1, blocking collectives: 7.07 us -> 70.9 us  [on_device(): every_filter = lax.all_gather(filters, 'chan', axis=1, tiled=True)]
    unnamed x14 -> x15, local copies, waits for them, and re-layouts: 16.7 us -> 35.3 us
    ppermute x0 -> x1, local copies, waits for them, and re-layouts: none -> 14.2 us  [apply_the_slots(): a_now = ppermute(after, 'chan', z)]
  transfers between devices with their start and end apart: 5 -> 5, of which waited for: 4 -> 3; matrix products, arithmetic and copies ran while one was open for 27% -> 23% of each run, Pallas kernels for 0% -> 0%
where the time goes in v1:
time: 788 us; the launch traced here: 780 us
  matrix products  283 us (36%)
  local copies, waits for them, and re-layouts  143 us (18%)
  other arithmetic  136 us (17%)
  waiting for transfers between devices  126 us (16%)
  blocking collectives  70.9 us (9%)
  between operations  14.5 us (2%)
    conv_general_dilated x3, matrix products, conv_local(): lax.conv_general_dilated(extended[None], filters, (2, 2, 2), ((0, 0), (1,...  283 us
    select_n x1, other arithmetic, apply_the_slots(): after = jnp.where(z2 & r_now == 0, state_now, new)  112 us
    psum x1, waiting for transfers between devices, on_device(): summed = lax.psum(grad_filters, 'space')  86.3 us
    all_gather x1, blocking collectives, on_device(): every_filter = lax.all_gather(filters, 'chan', axis=1, tiled=True)  70.9 us
    conv_general_dilated x6, local copies, waits for them, and re-layouts, conv_local(): lax.conv_general_dilated(extended[None], filters, (2, 2, 2), ((0, 0), (1,...  48.8 us
    unnamed x15, local copies, waits for them, and re-layouts  35.3 us
    all_gather x1, waiting for transfers between devices, on_device(): piece = lax.all_gather(preact_grad, 'chan', axis=0, tiled=True)  33.4 us
    concatenate x1, other arithmetic, on_device(): extended = jnp.concatenate([below[:, None], volume], axis=1)  18.6 us
  transfers between devices with their start and end apart: 5, of which 3 were waited for; matrix products, arithmetic and copies ran while one was open for 23% of the time, Pallas kernels for 0%

profile of v1, /device:TPU:8, one launch (start us, length us, event | category | flops | bytes accessed | tf_op | source)
XLA Modules:
  0.0 779.8 jit_solution(6693386760902949660)
XLA Ops:
  7.2 2.4 slice_bitcast_fusion.3
  11.6 8.7 %copy.51 = f32[16,2,128,128]{0,3,2,1:T(8,128)} copy(f32[16,2,128,128]{3,2,1,0:T(8,128)S(1)} %copy-done) | data formatting | bytes 4194304 | tf_op args[0]
  20.2 6.6 collective-permute-done
  26.9 4.6 copy.50
  31.5 18.6 %pad_maximum_fusion = f32[16,3,128,128]{0,3,2,1:T(8,128)} fusion(f32[16,2,128,128]{0,3,2,1:T(8,128)} %copy.51, f32[16,1,128,128]{0,3,2,1:T(8,128)} %bitcast.50), kind=kLoop, calls=%fused_computation.7 | loop fusion | flops 786432 | bytes 6291456 | tf_op jit(solution)/shard_map/concatenate | solution.py:51
  50.1 16.1 %copy.52 = f32[16,3,128,128]{3,2,1,0:T(8,128)} copy(f32[16,3,128,128]{0,3,2,1:T(8,128)} %pad_maximum_fusion) | data formatting | bytes 6291456 | tf_op jit(solution)/shard_map/concatenate | solution.py:51
  68.6 70.9 %all_gather.6 = f32[64,32,3,3,3]{0,1,4,3,2:T(8,128)S(1)} all-gather(f32[64,16,3,3,3]{0,1,4,3,2:T(8,128)S(1)} %copy-done.2), channel_id=1, replica_groups=mesh['space'=16,'chan'=2] {'chan'}, dimensions={1}, use_global_device_ids=true | all-gather | bytes 331776 | tf_op jit(solution)/shard_map/all_gather | solution.py:52
  139.5 14.2 %copy.53 = f32[16,3,128,128]{0,3,2,1:T(8,128)} copy(f32[16,3,128,128]{3,2,1,0:T(8,128)} %collective-permute-done.1) | data formatting | bytes 6291456 | tf_op jit(solution)/shard_map/ppermute | solution.py:18
  153.7 111.5 %broadcast_select_fusion = f32[1,32,3,128,128]{1,0,4,3,2:T(1,128)} fusion(pred[]{:T(512)S(6)} %eq.3, f32[1,16,3,128,128]{1,0,4,3,2:T(1,128)} %bitcast.48, f32[1,16,3,128,128]{1,0,4,3,2:T(1,128)} %bitcast.46), kind=kLoop, calls=%fused_computation | loop fusion | flops 4718592 | bytes 12582913 | tf_op jit(solution)/shard_map/jit(_where)/select_n | solution.py:21
  265.2 19.6 %copy.70 = f32[32,3,128,1,128]{2,0,4,1,3:T(8,128)} copy(f32[32,3,128,1,128]{0,4,2,1,3:T(8,128)} %bitcast.49) | data formatting | bytes 12582912
  284.8 6.7 pad.2.clone
  291.6 24.8 %copy.56 = f32[32,3,128,1,8,18]{0,4,5,2,1,3:T(8,128)} copy(f32[32,3,128,1,8,18]{2,0,5,4,1,3:T(8,128)} %bitcast.51) | data formatting | bytes 14155776 | tf_op jit(solution)/shard_map/conv_general_dilated | solution.py:36
  318.6 37.6 %fusion.11 = f32[1,64,8,9,32]{4,2,3,1,0:T(8,128)} fusion(f32[32,3,128,1,7,2]{0,4,5,2,1,3:T(8,128)S(1)} %slice.45, f32[32,3,128,1,8,18]{0,4,5,2,1,3:T(8,128)} %copy.56, pred[8,9]{0,1:T(8,128)(4,1)S(1)} %copy-done.4, f32[64,32,3,3,3]{0,1,4,3,2:T(8,128)S(1)} %all_gather.6, s32[]{:T(128)S(6)} %select_n.32), kind=kOutput, calls=%fused_computation.18 | convolution fusion | flops 1526906880 | bytes 8577100 | tf_op jit(solution)/shard_map/conv_general_dilated | solution.py:36
  361.8 33.4 %all-gather.2.cloned.1.call-done = f32[64,1,64,64]{3,2,1,0:T(8,128)} async-done(((f32[32,1,64,64]{3,2,1,0:T(8,128)}), f32[64,1,64,64]{3,2,1,0:T(8,128)}) %all-gather.2.cloned.1.call-update) | async-done | bytes 1048592 | tf_op jit(solution)/shard_map/all_gather | solution.py:61
  395.3 3.1 copy.61
  403.1 86.3 %broadcast_select_fusion.1 = f32[3,128,8,18,16]{4,2,3,1,0:T(8,128)} fusion(pred[8,18]{0,1:T(8,128)(4,1)S(1)} %copy-done.3, f32[64,16,3,3,3]{0,1,4,3,2:T(8,128)S(1)} %copy-done.2, f32[64,1,64,8,10]{0,3,4,2,1:T(8,128)S(1)} %fusion.32), kind=kOutput, calls=%fused_computation.10 | convolution fusion | flops 1521745920 | bytes 4960400 | tf_op jit(solution)/shard_map/transpose(jvp())/conv_general_dilated | solution.py:36
  489.5 17.2 %copy.64 = f32[3,128,8,18,16]{1,4,3,2,0:T(8,128)} copy(f32[3,128,8,18,16]{4,2,3,1,0:T(8,128)} %broadcast_select_fusion.1) | data formatting | bytes 7077888 | tf_op jit(solution)/shard_map/transpose(jvp())/conv_general_dilated | solution.py:36
  510.0 2.8 collective-permute-start.2
  512.8 3.3 copy.65
  516.1 159.1 %fusion.25 = f32[64,16,3,3,3]{0,1,4,3,2:T(8,128)} fusion(f32[1,16,3,128,128]{1,0,4,3,2:T(1,128)} %bitcast.47, f32[1,64,1,64,64]{1,0,4,3,2:T(1,128)} %bitcast.56), kind=kOutput, calls=%fused_computation.36 | convolution fusion | flops 1344835584 | bytes 4304896 | tf_op jit(solution)/shard_map/transpose(jvp())/conv_general_dilated | solution.py:36
  675.2 2.7 copy.66
  679.4 86.3 %all-reduce.2.cloned.1.call-done = f32[64,16,3,3,3]{0,1,4,3,2:T(8,128)} async-done(((f32[64,16,3,3,3]{0,1,4,3,2:T(8,128)}), f32[64,16,3,3,3]{0,1,4,3,2:T(8,128)}) %all-reduce.2.cloned.1.call-update) | async-done | bytes 110608 | tf_op jit(solution)/shard_map/psum | solution.py:74
  767.4 2.4 fusion.16
  769.7 2.9 copy.67
  (31 shorter events, 23.3 us)
Async XLA Ops:
  7.2 4.4 copy-start
  7.2 388.1 %all-gather.2.cloned.1.call-start = ((), (), s32[]{:S(2)}) async-start(), calls=%async_computation | async-start | bytes 3145728 | tf_op jit(solution)/shard_map/all_gather | solution.py:61
  9.7 17.2 %collective-permute-start = (f32[16,128,128]{2,1,0:T(8,128)}, f32[16,128,128]{2,1,0:T(8,128)S(1)}, u32[]{:S(2)}, u32[]{:S(2)}) collective-permute-start(f32[16,128,128]{2,1,0:T(8,128)} %slice_bitcast_fusion.3), channel_id=1, source_target_pairs={{0,2},{2,4},{4,6},{6,8},{8,10},{10,12},{12,14},{14,16},{16,18},{18... | collective-permute-start | bytes 3145736 | tf_op jit(solution)/shard_map/ppermute | solution.py:32
  50.1 17.6 %copy-start.1 = (f32[32,1,64,64]{3,2,1,0:T(8,128)S(1)}, f32[32,1,64,64]{3,2,1,0:T(8,128)}, u32[]{:S(2)}) copy-start(f32[32,1,64,64]{3,2,1,0:T(8,128)} %param.7) | copy-start | bytes 1572868
  50.1 18.5 %copy-start.2 = (f32[64,16,3,3,3]{0,1,4,3,2:T(8,128)S(1)}, f32[64,16,3,3,3]{0,1,4,3,2:T(8,128)}, u32[]{:S(2)}) copy-start(f32[64,16,3,3,3]{0,1,4,3,2:T(8,128)} %param.6) | copy-start | bytes 331780
  66.1 73.3 %collective-permute-start.1 = (f32[16,3,128,128]{3,2,1,0:T(8,128)}, f32[16,3,128,128]{3,2,1,0:T(8,128)}, u32[]{:S(2)}, u32[]{:S(2)}) collective-permute-start(f32[16,3,128,128]{3,2,1,0:T(8,128)} %copy.52), channel_id=1, source_target_pairs={{0,1},{1,0},{2,3},{3,2},{4,5},{5,4},{6,7},{7,6},{8,9},{9,8},{10,11... | collective-permute-start | bytes 9437192 | tf_op jit(solution)/shard_map/ppermute | solution.py:18
  316.3 2.2 copy-start.4
  361.8 403.9 %all-reduce.2.cloned.1.call-start = ((), (), s32[]{:S(2)}) async-start(), calls=%async_computation.1 | async-start | bytes 442368 | tf_op jit(solution)/shard_map/psum | solution.py:74
  402.5 0.7 copy-start.3
  510.0 257.4 %collective-permute-start.2 = (f32[16,128,128]{1,0,2:T(8,128)}, f32[16,128,128]{1,0,2:T(8,128)}, u32[]{:S(2)}, u32[]{:S(2)}) collective-permute-start(f32[16,128,128]{1,0,2:T(8,128)} %slice_bitcast_fusion.1), channel_id=1, source_target_pairs={{2,0},{4,2},{6,4},{8,6},{10,8},{12,10},{14,12},{16,14},{18,16},{20... | collective-permute-start | bytes 3145736 | tf_op jit(solution)/shard_map/ppermute | solution.py:32
Sparse Core Ops, SparseCore 0:
  361.9 33.3 all-gather.1
  675.3 90.3 all-reduce.1
